TPU v7x, 128 devices: a whole 4x4x4 slice. The times are simulated.
128 devices in a mesh: section: 8 (over x, core), space: 16 (over y, z).
Axes of the slice: x: 4, y: 4, z: 4, core: 2. Of those that a mesh axis runs over, the one named last changes fastest.
Arguments:
- features: bfloat16 [8, 2, 256, 1024], P(None, None, 'space'), may hold values from -6 to 6
- lift_w: bfloat16 [2, 32], replicated, may hold values from -4 to 4
- spec_w: bfloat16 [8, 64, 128, 32, 64], P('section', 'space'), may hold values from -3 to 3
- point_w: bfloat16 [8, 32, 32], P('section'), may hold values from -1.5 to 1.5
- point_b: bfloat16 [8, 32], P('section'), may hold values from -3 to 3
Outputs:
- saved: bfloat16 [8, 8, 32, 256, 1024], P('section', None, None, 'space')
All inputs are finite; a program needn't handle non-finite values.
Results may differ from a plain program's by a relative error of at most 0.03.
Values may be sent and summed in bfloat16 or wider, within the bound.
A program may use at most 128 MiB of HBM per device.

v0:
```python
import jax
import jax.numpy as jnp
from jax import lax
from jax.sharding import PartitionSpec as P


def from_behind(value, axis, by):
    size = lax.axis_size(axis)
    pairs = [(i, i + by) for i in range(size) if 0 <= i + by < size]
    return lax.ppermute(value, axis, pairs)


def turn_table(first, second, period):
    product = first[:, None] * second[None, :] % period
    return 2.0 * jnp.pi * product.astype(jnp.float32) / period


def row_freqs(height, modes_h):
    index = jnp.arange(modes_h, dtype=jnp.int32)
    return jnp.where(index < modes_h // 2, index, height - modes_h + index)


def fwd_w_table(cols, modes_w):
    column = jnp.arange(cols, dtype=jnp.int32)
    slot = jnp.arange(2 * modes_w, dtype=jnp.int32)
    angle = turn_table(column, slot // 2, cols)
    return jnp.where(slot[None, :] % 2 == 0, jnp.cos(angle), -jnp.sin(angle)).astype(jnp.bfloat16)


def fwd_h_table(height, modes_h):
    angle = turn_table(jnp.arange(height, dtype=jnp.int32), row_freqs(height, modes_h), height)
    return jnp.concatenate([jnp.cos(angle), jnp.sin(angle)], axis=1).astype(jnp.bfloat16)


def inv_h_table(height, modes_h):
    angle = turn_table(row_freqs(height, modes_h), jnp.arange(height, dtype=jnp.int32), height)
    cosine = jnp.cos(angle) / height
    sine = jnp.sin(angle) / height
    upper = jnp.concatenate([cosine, sine], axis=1)
    lower = jnp.concatenate([-sine, cosine], axis=1)
    return jnp.concatenate([upper, lower], axis=0).astype(jnp.bfloat16)


def inv_w_table(cols, modes_w):
    slot = jnp.arange(2 * modes_w, dtype=jnp.int32)
    mode = slot // 2
    angle = turn_table(mode, jnp.arange(cols, dtype=jnp.int32), cols)
    factor = jnp.where(mode == 0, 1.0, 2.0).astype(jnp.float32)[:, None] / cols
    return jnp.where(
        slot[:, None] % 2 == 0, factor * jnp.cos(angle), -factor * jnp.sin(angle)
    ).astype(jnp.bfloat16)


def on_device(features, lift_w, spec_w, point_w, point_b):
    space_count = lax.axis_size("space")
    section_count = lax.axis_size("section")
    section_pos = lax.axis_index("section")
    micro_count = features.shape[0]
    row_count = features.shape[2]
    col_count = features.shape[3]
    channels = lift_w.shape[1]
    local_modes = spec_w.shape[1]
    modes_h = spec_w.shape[2]
    modes_w = local_modes * space_count
    height = row_count * space_count
    fw_tab = fwd_w_table(col_count, modes_w)
    eh_tab = fwd_h_table(height, modes_h)
    gi_tab = inv_h_table(height, modes_h)
    gw_tab = inv_w_table(col_count, modes_w)

    def one_layer(field, weights, gain_w, bias):
        upart = jnp.einsum("crw,wk->krc", field, fw_tab, preferred_element_type=jnp.float32).astype(
            jnp.bfloat16
        )
        upart = upart.reshape(2 * modes_w, row_count * channels)
        columns = lax.all_to_all(upart, "space", split_axis=0, concat_axis=1, tiled=True)
        columns = columns.reshape(2 * local_modes, height, channels)
        proj = jnp.einsum("khc,hf->kcf", columns, eh_tab, preferred_element_type=jnp.float32)
        proj = proj.reshape(local_modes, 2, channels, 2 * modes_h)
        spec_re = (proj[:, 0, :, :modes_h] + proj[:, 1, :, modes_h:]).astype(jnp.bfloat16)
        spec_im = (proj[:, 1, :, :modes_h] - proj[:, 0, :, modes_h:]).astype(jnp.bfloat16)
        mixed_re = jnp.einsum("jcf,jfco->jfo", spec_re, weights, preferred_element_type=jnp.float32)
        mixed_im = jnp.einsum("jcf,jfco->jfo", spec_im, weights, preferred_element_type=jnp.float32)
        out_re = (mixed_re[..., :channels] - mixed_im[..., channels:]).astype(jnp.bfloat16)
        out_im = (mixed_re[..., channels:] + mixed_im[..., :channels]).astype(jnp.bfloat16)
        stacked = jnp.stack([out_re, out_im], axis=1).reshape(local_modes, 2 * modes_h, channels)
        zpart = jnp.einsum("jmc,mn->jnc", stacked, gi_tab, preferred_element_type=jnp.float32)
        zpart = zpart.astype(jnp.bfloat16).reshape(2 * local_modes, height * channels)
        back = lax.all_to_all(zpart, "space", split_axis=1, concat_axis=0, tiled=True)
        back = back.reshape(2 * modes_w, row_count, channels)
        spec = jnp.einsum("krc,kw->crw", back, gw_tab, preferred_element_type=jnp.float32)
        point = jnp.einsum("crw,co->orw", field, gain_w, preferred_element_type=jnp.float32)
        return jax.nn.gelu(spec + point + bias[:, None, None], approximate=True).astype(
            jnp.bfloat16
        )

    start_saved = jnp.zeros((micro_count, channels, row_count, col_count), jnp.bfloat16)
    own_weights = spec_w[0]
    own_gain = point_w[0]
    own_bias = point_b[0].astype(jnp.float32)

    def advance(tick, received, saved):
        entry = jnp.clip(tick, 0, micro_count - 1)
        grid_in = lax.dynamic_index_in_dim(features, entry, 0, keepdims=False)
        lifted = jnp.einsum(
            "frw,fc->crw", grid_in, lift_w, preferred_element_type=jnp.float32
        ).astype(jnp.bfloat16)
        incoming = jnp.where(section_pos == 0, lifted, received)
        result = one_layer(incoming, own_weights, own_gain, own_bias)
        micro_pos = tick - section_pos
        valid = (micro_pos >= 0) & (micro_pos < micro_count)
        target = jnp.clip(micro_pos, 0, micro_count - 1)
        previous = lax.dynamic_index_in_dim(saved, target, 0, keepdims=False)
        saved = lax.dynamic_update_index_in_dim(
            saved, jnp.where(valid, result, previous), target, 0
        )
        return (result, saved)

    def step(tick, carry):
        received, saved = carry
        result, saved = advance(tick, received, saved)
        received = from_behind(result, "section", 1)
        return (received, saved)

    start_field = jnp.zeros((channels, row_count, col_count), jnp.bfloat16)
    last_tick = micro_count + section_count - 2
    received, saved = lax.fori_loop(0, last_tick, step, (start_field, start_saved))
    result, saved = advance(last_tick, received, saved)
    return saved[None]


def solution(mesh):
    in_specs = (
        P(None, None, "space", None),
        P(),
        P("section", "space", None, None, None),
        P("section", None, None),
        P("section", None),
    )
    out_specs = P("section", None, None, "space", None)
    return jax.shard_map(
        on_device, mesh=mesh, in_specs=in_specs, out_specs=out_specs, check_vma=False
    )
```

profile of v0, /device:TPU:10, one launch (start us, length us, event | category | flops | bytes accessed | tf_op | source)
XLA Modules:
  0.0 921.1 jit_solution(9294941959977761456)
XLA Ops:
  1.3 7.4 copy.43
  14.6 855.2 %while.18 = (s32[]{:T(128)}, bf16[32,16,1024]{2,0,1:T(8,128)(2,1)S(1)}, bf16[8,32,16,1024]{3,1,2,0:T(8,128)(2,1)}, pred[]{:T(512)}, bf16[8,2,16,1024]{3,1,2,0:T(...) while((s32[]{:T(128)}, ...), condition=%wide.region_1.2_spmd.clone.clone, body=%wide.region_0.1_spmd.clone.clone.sunk | while | flops 388628480 | bytes 26547580 | solution.py:127
  20.1 8.4 all-to-all-start
  28.5 6.4 all-to-all-done
  35.8 7.4 fusion.206
  45.6 5.1 all-to-all-start.1
  52.0 5.1 all-to-all-done.1
  64.6 14.4 %collective-permute-done = bf16[32,16,1024]{2,0,1:T(8,128)(2,1)S(1)} collective-permute-done((bf16[32,16,1024]{2,0,1:T(8,128)(2,1)}, bf16[32,16,1024]{2,0,1:T(8,128)(2,1)S(1)}, u32[]{:S(2)}, u32[]{:S(2)}) %collective-permute-start) | collective-permute-done | bytes 1048608 | tf_op jit(solution)/shard_map/while/body/eval_jaxpr/ppermute | solution.py:10
  89.3 6.4 all-to-all-done
  96.6 7.4 fusion.206
  112.8 5.1 all-to-all-done.1
  125.4 14.4 %collective-permute-done = bf16[32,16,1024]{2,0,1:T(8,128)(2,1)S(1)} collective-permute-done((bf16[32,16,1024]{2,0,1:T(8,128)(2,1)}, bf16[32,16,1024]{2,0,1:T(8,128)(2,1)S(1)}, u32[]{:S(2)}, u32[]{:S(2)}) %collective-permute-start) | collective-permute-done | bytes 1048608 | tf_op jit(solution)/shard_map/while/body/eval_jaxpr/ppermute | solution.py:10
  150.1 6.4 all-to-all-done
  157.4 7.4 fusion.206
  173.6 5.1 all-to-all-done.1
  186.2 14.4 %collective-permute-done = bf16[32,16,1024]{2,0,1:T(8,128)(2,1)S(1)} collective-permute-done((bf16[32,16,1024]{2,0,1:T(8,128)(2,1)}, bf16[32,16,1024]{2,0,1:T(8,128)(2,1)S(1)}, u32[]{:S(2)}, u32[]{:S(2)}) %collective-permute-start) | collective-permute-done | bytes 1048608 | tf_op jit(solution)/shard_map/while/body/eval_jaxpr/ppermute | solution.py:10
  210.9 6.4 all-to-all-done
  218.2 7.4 fusion.206
  234.4 5.1 all-to-all-done.1
  247.0 14.4 %collective-permute-done = bf16[32,16,1024]{2,0,1:T(8,128)(2,1)S(1)} collective-permute-done((bf16[32,16,1024]{2,0,1:T(8,128)(2,1)}, bf16[32,16,1024]{2,0,1:T(8,128)(2,1)S(1)}, u32[]{:S(2)}, u32[]{:S(2)}) %collective-permute-start) | collective-permute-done | bytes 1048608 | tf_op jit(solution)/shard_map/while/body/eval_jaxpr/ppermute | solution.py:10
  271.7 6.4 all-to-all-done
  279.0 7.4 fusion.206
  295.2 5.1 all-to-all-done.1
  307.8 14.4 %collective-permute-done = bf16[32,16,1024]{2,0,1:T(8,128)(2,1)S(1)} collective-permute-done((bf16[32,16,1024]{2,0,1:T(8,128)(2,1)}, bf16[32,16,1024]{2,0,1:T(8,128)(2,1)S(1)}, u32[]{:S(2)}, u32[]{:S(2)}) %collective-permute-start) | collective-permute-done | bytes 1048608 | tf_op jit(solution)/shard_map/while/body/eval_jaxpr/ppermute | solution.py:10
  332.6 6.4 all-to-all-done
  339.9 7.4 fusion.206
  356.1 5.1 all-to-all-done.1
  368.8 14.4 %collective-permute-done = bf16[32,16,1024]{2,0,1:T(8,128)(2,1)S(1)} collective-permute-done((bf16[32,16,1024]{2,0,1:T(8,128)(2,1)}, bf16[32,16,1024]{2,0,1:T(8,128)(2,1)S(1)}, u32[]{:S(2)}, u32[]{:S(2)}) %collective-permute-start) | collective-permute-done | bytes 1048608 | tf_op jit(solution)/shard_map/while/body/eval_jaxpr/ppermute | solution.py:10
  393.5 6.4 all-to-all-done
  400.8 7.4 fusion.206
  417.0 5.1 all-to-all-done.1
  429.7 14.4 %collective-permute-done = bf16[32,16,1024]{2,0,1:T(8,128)(2,1)S(1)} collective-permute-done((bf16[32,16,1024]{2,0,1:T(8,128)(2,1)}, bf16[32,16,1024]{2,0,1:T(8,128)(2,1)S(1)}, u32[]{:S(2)}, u32[]{:S(2)}) %collective-permute-start) | collective-permute-done | bytes 1048608 | tf_op jit(solution)/shard_map/while/body/eval_jaxpr/ppermute | solution.py:10
  454.4 6.4 all-to-all-done
  461.7 7.4 fusion.206
  477.9 5.1 all-to-all-done.1
  490.5 14.4 %collective-permute-done = bf16[32,16,1024]{2,0,1:T(8,128)(2,1)S(1)} collective-permute-done((bf16[32,16,1024]{2,0,1:T(8,128)(2,1)}, bf16[32,16,1024]{2,0,1:T(8,128)(2,1)S(1)}, u32[]{:S(2)}, u32[]{:S(2)}) %collective-permute-start) | collective-permute-done | bytes 1048608 | tf_op jit(solution)/shard_map/while/body/eval_jaxpr/ppermute | solution.py:10
  510.2 5.1 all-to-all-start
  515.3 6.4 all-to-all-done
  522.6 7.4 fusion.206
  538.8 5.1 all-to-all-done.1
  551.4 14.4 %collective-permute-done = bf16[32,16,1024]{2,0,1:T(8,128)(2,1)S(1)} collective-permute-done((bf16[32,16,1024]{2,0,1:T(8,128)(2,1)}, bf16[32,16,1024]{2,0,1:T(8,128)(2,1)S(1)}, u32[]{:S(2)}, u32[]{:S(2)}) %collective-permute-start) | collective-permute-done | bytes 1048608 | tf_op jit(solution)/shard_map/while/body/eval_jaxpr/ppermute | solution.py:10
  576.1 6.4 all-to-all-done
  583.4 7.4 fusion.206
  599.6 5.1 all-to-all-done.1
  612.2 14.4 %collective-permute-done = bf16[32,16,1024]{2,0,1:T(8,128)(2,1)S(1)} collective-permute-done((bf16[32,16,1024]{2,0,1:T(8,128)(2,1)}, bf16[32,16,1024]{2,0,1:T(8,128)(2,1)S(1)}, u32[]{:S(2)}, u32[]{:S(2)}) %collective-permute-start) | collective-permute-done | bytes 1048608 | tf_op jit(solution)/shard_map/while/body/eval_jaxpr/ppermute | solution.py:10
  636.9 6.4 all-to-all-done
  644.2 7.4 fusion.206
  660.4 5.1 all-to-all-done.1
  673.0 14.4 %collective-permute-done = bf16[32,16,1024]{2,0,1:T(8,128)(2,1)S(1)} collective-permute-done((bf16[32,16,1024]{2,0,1:T(8,128)(2,1)}, bf16[32,16,1024]{2,0,1:T(8,128)(2,1)S(1)}, u32[]{:S(2)}, u32[]{:S(2)}) %collective-permute-start) | collective-permute-done | bytes 1048608 | tf_op jit(solution)/shard_map/while/body/eval_jaxpr/ppermute | solution.py:10
  697.7 6.4 all-to-all-done
  705.0 7.4 fusion.206
  721.2 5.1 all-to-all-done.1
  733.8 14.4 %collective-permute-done = bf16[32,16,1024]{2,0,1:T(8,128)(2,1)S(1)} collective-permute-done((bf16[32,16,1024]{2,0,1:T(8,128)(2,1)}, bf16[32,16,1024]{2,0,1:T(8,128)(2,1)S(1)}, u32[]{:S(2)}, u32[]{:S(2)}) %collective-permute-start) | collective-permute-done | bytes 1048608 | tf_op jit(solution)/shard_map/while/body/eval_jaxpr/ppermute | solution.py:10
  758.5 6.4 all-to-all-done
  765.9 7.4 fusion.206
  782.0 5.1 all-to-all-done.1
  794.6 14.4 %collective-permute-done = bf16[32,16,1024]{2,0,1:T(8,128)(2,1)S(1)} collective-permute-done((bf16[32,16,1024]{2,0,1:T(8,128)(2,1)}, bf16[32,16,1024]{2,0,1:T(8,128)(2,1)S(1)}, u32[]{:S(2)}, u32[]{:S(2)}) %collective-permute-start) | collective-permute-done | bytes 1048608 | tf_op jit(solution)/shard_map/while/body/eval_jaxpr/ppermute | solution.py:10
  819.3 6.4 all-to-all-done
  826.7 7.4 fusion.206
  842.8 5.1 all-to-all-done.1
  855.4 14.4 %collective-permute-done = bf16[32,16,1024]{2,0,1:T(8,128)(2,1)S(1)} collective-permute-done((bf16[32,16,1024]{2,0,1:T(8,128)(2,1)}, bf16[32,16,1024]{2,0,1:T(8,128)(2,1)S(1)}, u32[]{:S(2)}, u32[]{:S(2)}) %collective-permute-start) | collective-permute-done | bytes 1048608 | tf_op jit(solution)/shard_map/while/body/eval_jaxpr/ppermute | solution.py:10
  874.4 11.2 %all_to_all.106 = bf16[16,8,512]{2,1,0:T(8,128)(2,1)S(1)} all-to-all(bf16[16,8,512]{2,1,0:T(8,128)(2,1)S(1)} %all_to_all.76), channel_id=1, replica_groups=mesh['section'=8,'space'=16] {'space'}, dimensions={0} | all-to-all | bytes 262144 | tf_op jit(solution)/shard_map/all_to_all | solution.py:76
  886.6 7.4 fusion.78
  901.6 12.1 %copy.109 = bf16[8,32,16,1024]{3,2,1,0:T(8,128)(2,1)} copy(bf16[8,32,16,1024]{3,1,2,0:T(8,128)(2,1)} %get-tuple-element.277) | data formatting | bytes 16777216 | tf_op jit(solution)/shard_map/while | solution.py:127
  (441 shorter events, 395.8 us)
Async XLA Ops:
  1.2 7.5 copy-start
  1.2 8.8 copy-start.3
  1.2 8.8 copy-start.2
  10.2 4.4 copy-start.1
  20.1 14.8 %all-to-all-start = ((bf16[16,8,512]{2,1,0:T(8,128)(2,1)}), bf16[16,8,512]{2,1,0:T(8,128)(2,1)S(1)}, u32[]{:S(2)}, u32[]{:S(2)}) async-start(bf16[16,8,512]{2,1,0:T(8,128)(2,1)} %all_to_all.98), calls=%async_computation | async-start | bytes 262144 | tf_op jit(solution)/shard_map/while/body/eval_jaxpr/all_to_all | solution.py:76
  45.6 11.4 %all-to-all-start.1 = ((bf16[8,16,512]{2,0,1:T(8,128)(2,1)}), bf16[8,16,512]{2,0,1:T(8,128)(2,1)S(1)}, u32[]{:S(2)}, u32[]{:S(2)}) async-start(bf16[8,16,512]{2,0,1:T(8,128)(2,1)} %copy.133), calls=%async_computation.1 | async-start | bytes 262144 | tf_op jit(solution)/shard_map/while/body/eval_jaxpr/all_to_all | solution.py:89
  62.7 16.3 %collective-permute-start = (bf16[32,16,1024]{2,0,1:T(8,128)(2,1)}, bf16[32,16,1024]{2,0,1:T(8,128)(2,1)S(1)}, u32[]{:S(2)}, u32[]{:S(2)}) collective-permute-start(bf16[32,16,1024]{2,0,1:T(8,128)(2,1)} %get-tuple-element.585), channel_id=1, source_target_pairs={{0,16},{16,32},{32,48},{48,64},{64,80},{80,96},{96,112},{1,17},{17... | collective-permute-start | bytes 3145736 | tf_op jit(solution)/shard_map/while/body/eval_jaxpr/ppermute | solution.py:10
  84.2 11.4 %all-to-all-start = ((bf16[16,8,512]{2,1,0:T(8,128)(2,1)}), bf16[16,8,512]{2,1,0:T(8,128)(2,1)S(1)}, u32[]{:S(2)}, u32[]{:S(2)}) async-start(bf16[16,8,512]{2,1,0:T(8,128)(2,1)} %all_to_all.98), calls=%async_computation | async-start | bytes 262144 | tf_op jit(solution)/shard_map/while/body/eval_jaxpr/all_to_all | solution.py:76
  106.4 11.4 %all-to-all-start.1 = ((bf16[8,16,512]{2,0,1:T(8,128)(2,1)}), bf16[8,16,512]{2,0,1:T(8,128)(2,1)S(1)}, u32[]{:S(2)}, u32[]{:S(2)}) async-start(bf16[8,16,512]{2,0,1:T(8,128)(2,1)} %copy.133), calls=%async_computation.1 | async-start | bytes 262144 | tf_op jit(solution)/shard_map/while/body/eval_jaxpr/all_to_all | solution.py:89
  123.4 16.3 %collective-permute-start = (bf16[32,16,1024]{2,0,1:T(8,128)(2,1)}, bf16[32,16,1024]{2,0,1:T(8,128)(2,1)S(1)}, u32[]{:S(2)}, u32[]{:S(2)}) collective-permute-start(bf16[32,16,1024]{2,0,1:T(8,128)(2,1)} %get-tuple-element.585), channel_id=1, source_target_pairs={{0,16},{16,32},{32,48},{48,64},{64,80},{80,96},{96,112},{1,17},{17... | collective-permute-start | bytes 3145736 | tf_op jit(solution)/shard_map/while/body/eval_jaxpr/ppermute | solution.py:10
  145.0 11.4 %all-to-all-start = ((bf16[16,8,512]{2,1,0:T(8,128)(2,1)}), bf16[16,8,512]{2,1,0:T(8,128)(2,1)S(1)}, u32[]{:S(2)}, u32[]{:S(2)}) async-start(bf16[16,8,512]{2,1,0:T(8,128)(2,1)} %all_to_all.98), calls=%async_computation | async-start | bytes 262144 | tf_op jit(solution)/shard_map/while/body/eval_jaxpr/all_to_all | solution.py:76
  167.2 11.4 %all-to-all-start.1 = ((bf16[8,16,512]{2,0,1:T(8,128)(2,1)}), bf16[8,16,512]{2,0,1:T(8,128)(2,1)S(1)}, u32[]{:S(2)}, u32[]{:S(2)}) async-start(bf16[8,16,512]{2,0,1:T(8,128)(2,1)} %copy.133), calls=%async_computation.1 | async-start | bytes 262144 | tf_op jit(solution)/shard_map/while/body/eval_jaxpr/all_to_all | solution.py:89
  184.2 16.3 %collective-permute-start = (bf16[32,16,1024]{2,0,1:T(8,128)(2,1)}, bf16[32,16,1024]{2,0,1:T(8,128)(2,1)S(1)}, u32[]{:S(2)}, u32[]{:S(2)}) collective-permute-start(bf16[32,16,1024]{2,0,1:T(8,128)(2,1)} %get-tuple-element.585), channel_id=1, source_target_pairs={{0,16},{16,32},{32,48},{48,64},{64,80},{80,96},{96,112},{1,17},{17... | collective-permute-start | bytes 3145736 | tf_op jit(solution)/shard_map/while/body/eval_jaxpr/ppermute | solution.py:10
  205.8 11.4 %all-to-all-start = ((bf16[16,8,512]{2,1,0:T(8,128)(2,1)}), bf16[16,8,512]{2,1,0:T(8,128)(2,1)S(1)}, u32[]{:S(2)}, u32[]{:S(2)}) async-start(bf16[16,8,512]{2,1,0:T(8,128)(2,1)} %all_to_all.98), calls=%async_computation | async-start | bytes 262144 | tf_op jit(solution)/shard_map/while/body/eval_jaxpr/all_to_all | solution.py:76
  228.0 11.4 %all-to-all-start.1 = ((bf16[8,16,512]{2,0,1:T(8,128)(2,1)}), bf16[8,16,512]{2,0,1:T(8,128)(2,1)S(1)}, u32[]{:S(2)}, u32[]{:S(2)}) async-start(bf16[8,16,512]{2,0,1:T(8,128)(2,1)} %copy.133), calls=%async_computation.1 | async-start | bytes 262144 | tf_op jit(solution)/shard_map/while/body/eval_jaxpr/all_to_all | solution.py:89
  245.1 16.3 %collective-permute-start = (bf16[32,16,1024]{2,0,1:T(8,128)(2,1)}, bf16[32,16,1024]{2,0,1:T(8,128)(2,1)S(1)}, u32[]{:S(2)}, u32[]{:S(2)}) collective-permute-start(bf16[32,16,1024]{2,0,1:T(8,128)(2,1)} %get-tuple-element.585), channel_id=1, source_target_pairs={{0,16},{16,32},{32,48},{48,64},{64,80},{80,96},{96,112},{1,17},{17... | collective-permute-start | bytes 3145736 | tf_op jit(solution)/shard_map/while/body/eval_jaxpr/ppermute | solution.py:10
  266.7 11.4 %all-to-all-start = ((bf16[16,8,512]{2,1,0:T(8,128)(2,1)}), bf16[16,8,512]{2,1,0:T(8,128)(2,1)S(1)}, u32[]{:S(2)}, u32[]{:S(2)}) async-start(bf16[16,8,512]{2,1,0:T(8,128)(2,1)} %all_to_all.98), calls=%async_computation | async-start | bytes 262144 | tf_op jit(solution)/shard_map/while/body/eval_jaxpr/all_to_all | solution.py:76
  288.8 11.4 %all-to-all-start.1 = ((bf16[8,16,512]{2,0,1:T(8,128)(2,1)}), bf16[8,16,512]{2,0,1:T(8,128)(2,1)S(1)}, u32[]{:S(2)}, u32[]{:S(2)}) async-start(bf16[8,16,512]{2,0,1:T(8,128)(2,1)} %copy.133), calls=%async_computation.1 | async-start | bytes 262144 | tf_op jit(solution)/shard_map/while/body/eval_jaxpr/all_to_all | solution.py:89
  305.9 16.3 %collective-permute-start = (bf16[32,16,1024]{2,0,1:T(8,128)(2,1)}, bf16[32,16,1024]{2,0,1:T(8,128)(2,1)S(1)}, u32[]{:S(2)}, u32[]{:S(2)}) collective-permute-start(bf16[32,16,1024]{2,0,1:T(8,128)(2,1)} %get-tuple-element.585), channel_id=1, source_target_pairs={{0,16},{16,32},{32,48},{48,64},{64,80},{80,96},{96,112},{1,17},{17... | collective-permute-start | bytes 3145736 | tf_op jit(solution)/shard_map/while/body/eval_jaxpr/ppermute | solution.py:10
  327.5 11.4 %all-to-all-start = ((bf16[16,8,512]{2,1,0:T(8,128)(2,1)}), bf16[16,8,512]{2,1,0:T(8,128)(2,1)S(1)}, u32[]{:S(2)}, u32[]{:S(2)}) async-start(bf16[16,8,512]{2,1,0:T(8,128)(2,1)} %all_to_all.98), calls=%async_computation | async-start | bytes 262144 | tf_op jit(solution)/shard_map/while/body/eval_jaxpr/all_to_all | solution.py:76
  349.7 11.4 %all-to-all-start.1 = ((bf16[8,16,512]{2,0,1:T(8,128)(2,1)}), bf16[8,16,512]{2,0,1:T(8,128)(2,1)S(1)}, u32[]{:S(2)}, u32[]{:S(2)}) async-start(bf16[8,16,512]{2,0,1:T(8,128)(2,1)} %copy.133), calls=%async_computation.1 | async-start | bytes 262144 | tf_op jit(solution)/shard_map/while/body/eval_jaxpr/all_to_all | solution.py:89
  366.9 16.3 %collective-permute-start = (bf16[32,16,1024]{2,0,1:T(8,128)(2,1)}, bf16[32,16,1024]{2,0,1:T(8,128)(2,1)S(1)}, u32[]{:S(2)}, u32[]{:S(2)}) collective-permute-start(bf16[32,16,1024]{2,0,1:T(8,128)(2,1)} %get-tuple-element.585), channel_id=1, source_target_pairs={{0,16},{16,32},{32,48},{48,64},{64,80},{80,96},{96,112},{1,17},{17... | collective-permute-start | bytes 3145736 | tf_op jit(solution)/shard_map/while/body/eval_jaxpr/ppermute | solution.py:10
  388.5 11.4 %all-to-all-start = ((bf16[16,8,512]{2,1,0:T(8,128)(2,1)}), bf16[16,8,512]{2,1,0:T(8,128)(2,1)S(1)}, u32[]{:S(2)}, u32[]{:S(2)}) async-start(bf16[16,8,512]{2,1,0:T(8,128)(2,1)} %all_to_all.98), calls=%async_computation | async-start | bytes 262144 | tf_op jit(solution)/shard_map/while/body/eval_jaxpr/all_to_all | solution.py:76
  410.6 11.4 %all-to-all-start.1 = ((bf16[8,16,512]{2,0,1:T(8,128)(2,1)}), bf16[8,16,512]{2,0,1:T(8,128)(2,1)S(1)}, u32[]{:S(2)}, u32[]{:S(2)}) async-start(bf16[8,16,512]{2,0,1:T(8,128)(2,1)} %copy.133), calls=%async_computation.1 | async-start | bytes 262144 | tf_op jit(solution)/shard_map/while/body/eval_jaxpr/all_to_all | solution.py:89
  427.7 16.3 %collective-permute-start = (bf16[32,16,1024]{2,0,1:T(8,128)(2,1)}, bf16[32,16,1024]{2,0,1:T(8,128)(2,1)S(1)}, u32[]{:S(2)}, u32[]{:S(2)}) collective-permute-start(bf16[32,16,1024]{2,0,1:T(8,128)(2,1)} %get-tuple-element.585), channel_id=1, source_target_pairs={{0,16},{16,32},{32,48},{48,64},{64,80},{80,96},{96,112},{1,17},{17... | collective-permute-start | bytes 3145736 | tf_op jit(solution)/shard_map/while/body/eval_jaxpr/ppermute | solution.py:10
  449.3 11.4 %all-to-all-start = ((bf16[16,8,512]{2,1,0:T(8,128)(2,1)}), bf16[16,8,512]{2,1,0:T(8,128)(2,1)S(1)}, u32[]{:S(2)}, u32[]{:S(2)}) async-start(bf16[16,8,512]{2,1,0:T(8,128)(2,1)} %all_to_all.98), calls=%async_computation | async-start | bytes 262144 | tf_op jit(solution)/shard_map/while/body/eval_jaxpr/all_to_all | solution.py:76
  471.5 11.4 %all-to-all-start.1 = ((bf16[8,16,512]{2,0,1:T(8,128)(2,1)}), bf16[8,16,512]{2,0,1:T(8,128)(2,1)S(1)}, u32[]{:S(2)}, u32[]{:S(2)}) async-start(bf16[8,16,512]{2,0,1:T(8,128)(2,1)} %copy.133), calls=%async_computation.1 | async-start | bytes 262144 | tf_op jit(solution)/shard_map/while/body/eval_jaxpr/all_to_all | solution.py:89
  488.6 16.3 %collective-permute-start = (bf16[32,16,1024]{2,0,1:T(8,128)(2,1)}, bf16[32,16,1024]{2,0,1:T(8,128)(2,1)S(1)}, u32[]{:S(2)}, u32[]{:S(2)}) collective-permute-start(bf16[32,16,1024]{2,0,1:T(8,128)(2,1)} %get-tuple-element.585), channel_id=1, source_target_pairs={{0,16},{16,32},{32,48},{48,64},{64,80},{80,96},{96,112},{1,17},{17... | collective-permute-start | bytes 3145736 | tf_op jit(solution)/shard_map/while/body/eval_jaxpr/ppermute | solution.py:10
  510.2 11.5 %all-to-all-start = ((bf16[16,8,512]{2,1,0:T(8,128)(2,1)}), bf16[16,8,512]{2,1,0:T(8,128)(2,1)S(1)}, u32[]{:S(2)}, u32[]{:S(2)}) async-start(bf16[16,8,512]{2,1,0:T(8,128)(2,1)} %all_to_all.98), calls=%async_computation | async-start | bytes 262144 | tf_op jit(solution)/shard_map/while/body/eval_jaxpr/all_to_all | solution.py:76
  532.4 11.4 %all-to-all-start.1 = ((bf16[8,16,512]{2,0,1:T(8,128)(2,1)}), bf16[8,16,512]{2,0,1:T(8,128)(2,1)S(1)}, u32[]{:S(2)}, u32[]{:S(2)}) async-start(bf16[8,16,512]{2,0,1:T(8,128)(2,1)} %copy.133), calls=%async_computation.1 | async-start | bytes 262144 | tf_op jit(solution)/shard_map/while/body/eval_jaxpr/all_to_all | solution.py:89
  549.5 16.3 %collective-permute-start = (bf16[32,16,1024]{2,0,1:T(8,128)(2,1)}, bf16[32,16,1024]{2,0,1:T(8,128)(2,1)S(1)}, u32[]{:S(2)}, u32[]{:S(2)}) collective-permute-start(bf16[32,16,1024]{2,0,1:T(8,128)(2,1)} %get-tuple-element.585), channel_id=1, source_target_pairs={{0,16},{16,32},{32,48},{48,64},{64,80},{80,96},{96,112},{1,17},{17... | collective-permute-start | bytes 3145736 | tf_op jit(solution)/shard_map/while/body/eval_jaxpr/ppermute | solution.py:10
  571.1 11.4 %all-to-all-start = ((bf16[16,8,512]{2,1,0:T(8,128)(2,1)}), bf16[16,8,512]{2,1,0:T(8,128)(2,1)S(1)}, u32[]{:S(2)}, u32[]{:S(2)}) async-start(bf16[16,8,512]{2,1,0:T(8,128)(2,1)} %all_to_all.98), calls=%async_computation | async-start | bytes 262144 | tf_op jit(solution)/shard_map/while/body/eval_jaxpr/all_to_all | solution.py:76
  593.2 11.4 %all-to-all-start.1 = ((bf16[8,16,512]{2,0,1:T(8,128)(2,1)}), bf16[8,16,512]{2,0,1:T(8,128)(2,1)S(1)}, u32[]{:S(2)}, u32[]{:S(2)}) async-start(bf16[8,16,512]{2,0,1:T(8,128)(2,1)} %copy.133), calls=%async_computation.1 | async-start | bytes 262144 | tf_op jit(solution)/shard_map/while/body/eval_jaxpr/all_to_all | solution.py:89
  610.3 16.3 %collective-permute-start = (bf16[32,16,1024]{2,0,1:T(8,128)(2,1)}, bf16[32,16,1024]{2,0,1:T(8,128)(2,1)S(1)}, u32[]{:S(2)}, u32[]{:S(2)}) collective-permute-start(bf16[32,16,1024]{2,0,1:T(8,128)(2,1)} %get-tuple-element.585), channel_id=1, source_target_pairs={{0,16},{16,32},{32,48},{48,64},{64,80},{80,96},{96,112},{1,17},{17... | collective-permute-start | bytes 3145736 | tf_op jit(solution)/shard_map/while/body/eval_jaxpr/ppermute | solution.py:10
  631.9 11.4 %all-to-all-start = ((bf16[16,8,512]{2,1,0:T(8,128)(2,1)}), bf16[16,8,512]{2,1,0:T(8,128)(2,1)S(1)}, u32[]{:S(2)}, u32[]{:S(2)}) async-start(bf16[16,8,512]{2,1,0:T(8,128)(2,1)} %all_to_all.98), calls=%async_computation | async-start | bytes 262144 | tf_op jit(solution)/shard_map/while/body/eval_jaxpr/all_to_all | solution.py:76
  654.0 11.4 %all-to-all-start.1 = ((bf16[8,16,512]{2,0,1:T(8,128)(2,1)}), bf16[8,16,512]{2,0,1:T(8,128)(2,1)S(1)}, u32[]{:S(2)}, u32[]{:S(2)}) async-start(bf16[8,16,512]{2,0,1:T(8,128)(2,1)} %copy.133), calls=%async_computation.1 | async-start | bytes 262144 | tf_op jit(solution)/shard_map/while/body/eval_jaxpr/all_to_all | solution.py:89
  671.1 16.3 %collective-permute-start = (bf16[32,16,1024]{2,0,1:T(8,128)(2,1)}, bf16[32,16,1024]{2,0,1:T(8,128)(2,1)S(1)}, u32[]{:S(2)}, u32[]{:S(2)}) collective-permute-start(bf16[32,16,1024]{2,0,1:T(8,128)(2,1)} %get-tuple-element.585), channel_id=1, source_target_pairs={{0,16},{16,32},{32,48},{48,64},{64,80},{80,96},{96,112},{1,17},{17... | collective-permute-start | bytes 3145736 | tf_op jit(solution)/shard_map/while/body/eval_jaxpr/ppermute | solution.py:10
  692.7 11.4 %all-to-all-start = ((bf16[16,8,512]{2,1,0:T(8,128)(2,1)}), bf16[16,8,512]{2,1,0:T(8,128)(2,1)S(1)}, u32[]{:S(2)}, u32[]{:S(2)}) async-start(bf16[16,8,512]{2,1,0:T(8,128)(2,1)} %all_to_all.98), calls=%async_computation | async-start | bytes 262144 | tf_op jit(solution)/shard_map/while/body/eval_jaxpr/all_to_all | solution.py:76
  714.8 11.4 %all-to-all-start.1 = ((bf16[8,16,512]{2,0,1:T(8,128)(2,1)}), bf16[8,16,512]{2,0,1:T(8,128)(2,1)S(1)}, u32[]{:S(2)}, u32[]{:S(2)}) async-start(bf16[8,16,512]{2,0,1:T(8,128)(2,1)} %copy.133), calls=%async_computation.1 | async-start | bytes 262144 | tf_op jit(solution)/shard_map/while/body/eval_jaxpr/all_to_all | solution.py:89
  731.9 16.3 %collective-permute-start = (bf16[32,16,1024]{2,0,1:T(8,128)(2,1)}, bf16[32,16,1024]{2,0,1:T(8,128)(2,1)S(1)}, u32[]{:S(2)}, u32[]{:S(2)}) collective-permute-start(bf16[32,16,1024]{2,0,1:T(8,128)(2,1)} %get-tuple-element.585), channel_id=1, source_target_pairs={{0,16},{16,32},{32,48},{48,64},{64,80},{80,96},{96,112},{1,17},{17... | collective-permute-start | bytes 3145736 | tf_op jit(solution)/shard_map/while/body/eval_jaxpr/ppermute | solution.py:10
  753.5 11.4 %all-to-all-start = ((bf16[16,8,512]{2,1,0:T(8,128)(2,1)}), bf16[16,8,512]{2,1,0:T(8,128)(2,1)S(1)}, u32[]{:S(2)}, u32[]{:S(2)}) async-start(bf16[16,8,512]{2,1,0:T(8,128)(2,1)} %all_to_all.98), calls=%async_computation | async-start | bytes 262144 | tf_op jit(solution)/shard_map/while/body/eval_jaxpr/all_to_all | solution.py:76
  775.7 11.4 %all-to-all-start.1 = ((bf16[8,16,512]{2,0,1:T(8,128)(2,1)}), bf16[8,16,512]{2,0,1:T(8,128)(2,1)S(1)}, u32[]{:S(2)}, u32[]{:S(2)}) async-start(bf16[8,16,512]{2,0,1:T(8,128)(2,1)} %copy.133), calls=%async_computation.1 | async-start | bytes 262144 | tf_op jit(solution)/shard_map/while/body/eval_jaxpr/all_to_all | solution.py:89
  792.7 16.3 %collective-permute-start = (bf16[32,16,1024]{2,0,1:T(8,128)(2,1)}, bf16[32,16,1024]{2,0,1:T(8,128)(2,1)S(1)}, u32[]{:S(2)}, u32[]{:S(2)}) collective-permute-start(bf16[32,16,1024]{2,0,1:T(8,128)(2,1)} %get-tuple-element.585), channel_id=1, source_target_pairs={{0,16},{16,32},{32,48},{48,64},{64,80},{80,96},{96,112},{1,17},{17... | collective-permute-start | bytes 3145736 | tf_op jit(solution)/shard_map/while/body/eval_jaxpr/ppermute | solution.py:10
  814.3 11.4 %all-to-all-start = ((bf16[16,8,512]{2,1,0:T(8,128)(2,1)}), bf16[16,8,512]{2,1,0:T(8,128)(2,1)S(1)}, u32[]{:S(2)}, u32[]{:S(2)}) async-start(bf16[16,8,512]{2,1,0:T(8,128)(2,1)} %all_to_all.98), calls=%async_computation | async-start | bytes 262144 | tf_op jit(solution)/shard_map/while/body/eval_jaxpr/all_to_all | solution.py:76
  836.5 11.4 %all-to-all-start.1 = ((bf16[8,16,512]{2,0,1:T(8,128)(2,1)}), bf16[8,16,512]{2,0,1:T(8,128)(2,1)S(1)}, u32[]{:S(2)}, u32[]{:S(2)}) async-start(bf16[8,16,512]{2,0,1:T(8,128)(2,1)} %copy.133), calls=%async_computation.1 | async-start | bytes 262144 | tf_op jit(solution)/shard_map/while/body/eval_jaxpr/all_to_all | solution.py:89
  853.5 16.3 %collective-permute-start = (bf16[32,16,1024]{2,0,1:T(8,128)(2,1)}, bf16[32,16,1024]{2,0,1:T(8,128)(2,1)S(1)}, u32[]{:S(2)}, u32[]{:S(2)}) collective-permute-start(bf16[32,16,1024]{2,0,1:T(8,128)(2,1)} %get-tuple-element.585), channel_id=1, source_target_pairs={{0,16},{16,32},{32,48},{48,64},{64,80},{80,96},{96,112},{1,17},{17... | collective-permute-start | bytes 3145736 | tf_op jit(solution)/shard_map/while/body/eval_jaxpr/ppermute | solution.py:10
  896.5 17.2 %all-to-all-start.3 = ((bf16[8,16,512]{2,0,1:T(8,128)(2,1)}), bf16[8,16,512]{2,0,1:T(8,128)(2,1)S(1)}, u32[]{:S(2)}, u32[]{:S(2)}) async-start(bf16[8,16,512]{2,0,1:T(8,128)(2,1)} %copy.53), calls=%async_computation.3 | async-start | bytes 262144 | tf_op jit(solution)/shard_map/all_to_all | solution.py:89
where the time goes:
time: 927 us; the launch traced here: 921 us
  waiting for transfers between devices  362 us (39%)
  starting transfers between devices  177 us (19%)
  matrix products  143 us (15%)
  other arithmetic  114 us (12%)
  local copies, waits for them, and re-layouts  112 us (12%)
  blocking collectives  11.2 us (1%)
    ppermute x14, waiting for transfers between devices, from_behind(): return lax.ppermute(value, axis, pairs)  202 us
    while x28, other arithmetic  104 us
    all_to_all x14, waiting for transfers between devices, one_layer(): lax.all_to_all(upart, 'space', split_axis=0, concat_axis=1, tiled=True)  89.5 us
    all_to_all x15, starting transfers between devices, one_layer(): lax.all_to_all(zpart, 'space', split_axis=1, concat_axis=0, tiled=True)  75.8 us
    all_to_all x14, starting transfers between devices, one_layer(): lax.all_to_all(upart, 'space', split_axis=0, concat_axis=1, tiled=True)  74.1 us
    all_to_all x15, waiting for transfers between devices, one_layer(): lax.all_to_all(zpart, 'space', split_axis=1, concat_axis=0, tiled=True)  71 us
    dot_general x15, matrix products, one_layer(): jnp.einsum('crw,co->orw', field, gain_w, preferred_element_type=jnp.float32)  40.1 us
    dot_general x14, matrix products, one_layer(): jnp.einsum('krc,kw->crw', back, gw_tab, preferred_element_type=jnp.float32)  37.1 us
  transfers between devices with their start and end apart: 43, of which 42 were waited for; matrix products, arithmetic and copies ran while one was open for 3% of the time, Pallas kernels for 0%

commit v1 on v0

v1 whole, which is shorter than its diff:
```python
import functools

import jax
import jax.numpy as jnp
import numpy as np
from jax import lax
from jax.experimental import pallas as pl
from jax.experimental.pallas import tpu as pltpu
from jax.sharding import PartitionSpec as P

MESH = pl.DeviceIdType.MESH
F32 = jnp.float32
BF16 = jnp.bfloat16

CH = 32
ROWS = 256
COLS = 1024
MW = 64
MH = 128
NSP = 16
NSEC = 8
LR = ROWS // NSP
LM = MW // NSP
W_ROWS = 4096 + 64


def make_tables():
    def tab(a, b, n, fn):
        return fn(2.0 * np.pi * ((a * b) % n) / n)

    bf = lambda x: np.asarray(x, np.float32).astype(BF16)
    freqs = np.where(np.arange(MH) < MH // 2, np.arange(MH), ROWS - MH + np.arange(MH))
    w = np.arange(COLS)
    q, part, j = np.meshgrid(np.arange(NSP), np.arange(2), np.arange(LM), indexing="ij")
    mode = (4 * q + j).reshape(-1)
    part = part.reshape(-1)
    cos = tab(mode[:, None], w[None], COLS, np.cos)
    sin = tab(mode[:, None], w[None], COLS, np.sin)
    fwt = bf(np.where(part[:, None] == 0, cos, -sin))
    s, ib, po, i8 = np.meshgrid(np.arange(2), np.arange(16), np.arange(2), np.arange(8), indexing="ij")
    s, po = s.reshape(-1), po.reshape(-1)
    f = freqs[(ib * 8 + i8).reshape(-1)]
    pt, hh, pp = np.meshgrid(np.arange(2), np.arange(LR), np.arange(NSP), indexing="ij")
    pt = pt.reshape(-1)
    h = (16 * pp + hh).reshape(-1)
    cos = tab(f[:, None], h[None], ROWS, np.cos)
    sin = tab(f[:, None], h[None], ROWS, np.sin)
    xr = np.where(pt[None] == 0, cos, sin)
    xi = np.where(pt[None] == 0, -sin, cos)
    sel = (s * 2 + po)[:, None]
    e2 = bf(np.select([sel == 0, sel == 1, sel == 2, sel == 3], [xr, xi, -xi, xr]))
    p_, hg, h4, q2 = np.meshgrid(np.arange(16), np.arange(4), np.arange(4), np.arange(2), indexing="ij")
    h = (16 * p_ + 4 * hg + h4).reshape(-1)
    q2 = q2.reshape(-1)
    ib, pi_, i8 = np.meshgrid(np.arange(16), np.arange(2), np.arange(8), indexing="ij")
    f = freqs[(ib * 8 + i8).reshape(-1)]
    pi_ = pi_.reshape(-1)
    cos = tab(h[:, None], f[None], ROWS, np.cos) / ROWS
    sin = tab(h[:, None], f[None], ROWS, np.sin) / ROWS
    sel = (pi_[None] * 2 + q2[:, None])
    gi = bf(np.select([sel == 0, sel == 1, sel == 2, sel == 3], [cos, sin, -sin, cos]))
    j, q, h4, q2 = np.meshgrid(np.arange(4), np.arange(16), np.arange(4), np.arange(2), indexing="ij")
    mode = (4 * q + j).reshape(-1)
    q2 = q2.reshape(-1)
    c = np.where(mode == 0, 1.0, 2.0)[:, None] / COLS
    gw = bf(np.where(q2[:, None] == 0, c * tab(mode[:, None], w[None], COLS, np.cos),
                     -c * tab(mode[:, None], w[None], COLS, np.sin)))
    perm = np.zeros((128, 128), np.float32)
    for k in range(8):
        for p in range(16):
            perm[k * 16 + p, p * 8 + k] = 1.0
    rep = np.zeros((128, 512), np.float32)
    for jj in range(4):
        for r in range(4):
            for cc in range(32):
                rep[jj * 32 + cc, jj * 128 + r * 32 + cc] = 1.0
    return fwt, e2, gi, gw, bf(perm), bf(rep)


def roll(x, amount):
    return x if amount % 128 == 0 else pltpu.roll(x, amount % 128, 1)


def chunk_of(shape):
    return lax.broadcasted_iota(jnp.int32, shape, 1) // 32


def by_chunk(parts):
    lane = chunk_of(parts[0].shape)
    out = parts[3]
    for j in (2, 1, 0):
        out = jnp.where(lane == j, parts[j], out)
    return out


def forward_w(fwt, field):
    return lax.dot_general(fwt, field, (((1,), (1,)), ((), ())), preferred_element_type=F32)


def gather_rows(perm, slabs, put):
    v = jnp.dot(perm, slabs, preferred_element_type=F32)
    for part in range(2):
        for hg in range(4):
            src = [
                v[(part * 4 + j) * 16 : (part * 4 + j + 1) * 16, hg * 128 : (hg + 1) * 128]
                for j in range(4)
            ]
            for g in range(4):
                row = (part * 16 + hg * 4 + g) * 16
                put(row, by_chunk([roll(src[j], 32 * (j - g)) for j in range(4)]).astype(BF16))


def spread(e2, rep, spectra):
    x = jnp.dot(e2, spectra, preferred_element_type=F32).astype(BF16)
    return jnp.dot(x, rep, preferred_element_type=F32).astype(BF16)


def mix_pair(get, weights):
    shape = (16, 128)
    row = lax.broadcasted_iota(jnp.int32, shape, 0) % 8
    lane = chunk_of(shape)
    zero = jnp.zeros(shape, BF16)
    rows = []
    for b in range(2):
        for j in range(4):
            blocks = []
            for s in range(2):
                x = get(s, b, j)
                for half in range(2):
                    blocks.append(jnp.where(row == lane + 4 * half, x, zero))
            rows.append(jnp.concatenate(blocks, axis=1))
    lhs = jnp.concatenate(rows, axis=0)
    out = jnp.dot(lhs, weights, preferred_element_type=F32)
    res = []
    for b in range(2):
        res.append(by_chunk([
            out[(b * 4 + j) * 16 : (b * 4 + j + 1) * 16, b * 128 : (b + 1) * 128] for j in range(4)
        ]))
    return jnp.concatenate(res, axis=0).astype(BF16)


def spread_rows(slabs, hg, put):
    t = slabs.T.astype(BF16)
    shape = (32, 128)
    lane = (lax.broadcasted_iota(jnp.int32, shape, 1) // 2) % 4
    zero = jnp.zeros(shape, BF16)
    for h4 in range(4):
        for j in range(4):
            put((hg * 4 + h4) * 32, j * 128, jnp.where(lane == h4, t[j * 32 : (j + 1) * 32], zero))


def gelu(x):
    inner = x * (0.7978845608028654 + 0.035677408136300125 * (x * x))
    half = 0.5 * x
    return half + half * jnp.tanh(inner)


def fused(feat, lift, w_all, fwt, e2, gi, gw, perm, rep, out, *scratch):
    (fields, wts, us, ur, zs, zr, rhs, xrep, y_s, lhs, kron,
     w_sem, u_ssem, u_rsem, z_ssem, z_rsem, o_ssem, o_rsem, o_lsem) = scratch
    sec = lax.axis_index("section")
    me = lax.axis_index("space")

    barrier = pltpu.get_barrier_semaphore()

    def greet_space(d, _):
        pl.semaphore_signal(barrier, inc=1, device_id={"section": sec, "space": lax.rem(me + d, NSP)}, device_id_type=MESH)
        return 0

    def greet_section(d, _):
        pl.semaphore_signal(barrier, inc=1, device_id={"section": lax.rem(sec + d, NSEC), "space": me}, device_id_type=MESH)
        return 0

    lax.fori_loop(1, NSP, greet_space, 0)
    lax.fori_loop(1, NSEC, greet_section, 0)

    def w_copy(l):
        return pltpu.make_async_copy(w_all.at[l], wts.at[l], w_sem.at[l])

    def start_w(l, _):
        w_copy(l).start()
        return 0

    lax.fori_loop(0, NSEC, start_w, 0)

    for r in range(4):
        fields[0, r * 128 : (r + 1) * 128, :] = jnp.dot(
            lift[r * 128 : (r + 1) * 128, :], feat[sec], preferred_element_type=F32
        ).astype(BF16)

    pl.semaphore_wait(barrier, NSP - 1 + NSEC - 1)

    def u_copy(l, peer):
        return pltpu.make_async_remote_copy(
            src_ref=us.at[l, peer], dst_ref=ur.at[l, me], send_sem=u_ssem.at[l], recv_sem=u_rsem.at[l],
            device_id={"section": sec, "space": peer}, device_id_type=MESH)

    def z_copy(l, peer):
        return pltpu.make_async_remote_copy(
            src_ref=zs.at[l, peer], dst_ref=zr.at[l, :, me], send_sem=z_ssem.at[l], recv_sem=z_rsem.at[l],
            device_id={"section": sec, "space": peer}, device_id_type=MESH)

    def u_all(l):
        return pltpu.make_async_remote_copy(
            src_ref=us.at[l, pl.ds(0, NSP - 1)], dst_ref=ur.at[l, pl.ds(0, NSP - 1)],
            send_sem=u_ssem.at[l], recv_sem=u_rsem.at[l],
            device_id={"section": sec, "space": lax.rem(me + 1, NSP)}, device_id_type=MESH)

    def z_all(l):
        return pltpu.make_async_remote_copy(
            src_ref=zs.at[l, pl.ds(0, NSP - 1)], dst_ref=zs.at[l, pl.ds(0, NSP - 1)],
            send_sem=z_ssem.at[l], recv_sem=z_rsem.at[l],
            device_id={"section": sec, "space": lax.rem(me + 1, NSP)}, device_id_type=MESH)

    def out_remote(l):
        return pltpu.make_async_remote_copy(
            src_ref=fields.at[l + 1], dst_ref=out.at[sec], send_sem=o_ssem.at[l], recv_sem=o_rsem.at[sec],
            device_id={"section": l, "space": me}, device_id_type=MESH)

    def out_local(l):
        return pltpu.make_async_copy(fields.at[l + 1], out.at[sec], o_lsem)

    def layer(l, _):
        u = forward_w(fwt[...], fields[l])
        us[l] = u.reshape(NSP, 8, 512).astype(BF16)

        def send_u(d, _):
            u_copy(l, lax.rem(me + d, NSP)).start()
            return 0

        lax.fori_loop(1, NSP, send_u, 0)
        ur[l, me] = us[l, me]
        u_all(l).wait_recv()

        def put_rhs(row, value):
            rhs[row : row + 16, :] = value

        gather_rows(perm[...], ur[l].reshape(128, 512), put_rhs)
        xrep[...] = spread(e2[...], rep[...], rhs[...])

        w_copy(l).wait()

        for ibp in range(8):
            def get(s, b, j, ibp=ibp):
                row = s * 256 + (2 * ibp + b) * 16
                return xrep[row : row + 16, j * 128 : (j + 1) * 128]

            y_s[ibp * 32 : (ibp + 1) * 32, :] = mix_pair(get, wts[l, ibp * 512 : (ibp + 1) * 512, :])

        z = jnp.dot(gi[...], y_s[...], preferred_element_type=F32)
        zs[l] = z.reshape(NSP, 4, 8, 128).astype(BF16)

        def send_z(d, _):
            z_copy(l, lax.rem(me + d, NSP)).start()
            return 0

        lax.fori_loop(1, NSP, send_z, 0)
        zr[l, :, me] = zs[l, me]

        wt = wts[l, 4096:4128, :]
        lane = chunk_of((32, 256))
        for h in range(8):
            kron[h * 32 : (h + 1) * 32, :] = jnp.where(lane == h, wt, jnp.zeros_like(wt))

        z_all(l).wait_recv()

        def put_lhs(row, col, value):
            lhs[row : row + 32, col : col + 128] = value

        for hg in range(4):
            spread_rows(zr[l, hg].astype(F32).reshape(128, 128), hg, put_lhs)

        bias = wts[l, 4128:4160, :].astype(F32)

        def tail(wc, _):
            cols = pl.ds(pl.multiple_of(wc * 256, 256), 256)
            spec = jnp.dot(lhs[...], gw[:, cols], preferred_element_type=F32)
            for rb in range(2):
                rows = slice(rb * 256, (rb + 1) * 256)
                x = spec[rows] + jnp.dot(kron[...], fields[l, rows, cols], preferred_element_type=F32)
                x = (x.reshape(8, 32, 256) + bias[None]).reshape(256, 256)
                fields[l + 1, rows, cols] = gelu(x).astype(BF16)
            return 0

        lax.fori_loop(0, 4, tail, 0)

        @pl.when(l == sec)
        def _():
            out_local(l).start()

        @pl.when(l != sec)
        def _():
            out_remote(l).start()

        return 0

    lax.fori_loop(0, NSEC, layer, 0)

    def finish(l, _):
        u_all(l).wait_send()
        z_all(l).wait_send()

        @pl.when(l == sec)
        def _():
            out_local(l).wait()

        @pl.when(l != sec)
        def _():
            out_remote(l).wait_send()
            pltpu.make_async_remote_copy(
                src_ref=fields.at[0], dst_ref=out.at[l], send_sem=o_ssem.at[l], recv_sem=o_rsem.at[l],
                device_id={"section": l, "space": me}, device_id_type=MESH).wait_recv()

        return 0

    lax.fori_loop(0, NSEC, finish, 0)


def pack_weights(spec_w, point_w, point_b):
    s = spec_w.reshape(LM, 8, 2, 8, CH, 2, CH)
    s = s.transpose(1, 5, 3, 4, 2, 0, 6).reshape(4096, 256)
    wt = jnp.tile(point_w.T, (1, 8))
    bias = jnp.broadcast_to(point_b[:, None], (CH, 256))
    return jnp.concatenate([s, wt, bias], axis=0)


def on_device(features, lift_w, spec_w, point_w, point_b):
    fwt, e2, gi, gw, perm, rep = make_tables()
    feat = features.reshape(NSEC, 2 * LR, COLS)
    eye = jnp.eye(LR, dtype=BF16)
    lift = (lift_w.T[None, :, :, None] * eye[:, None, None, :]).reshape(LR * CH, 2 * LR)
    own = pack_weights(spec_w[0], point_w[0], point_b[0])
    w_all = lax.all_gather(own, "section")
    vmem = pl.BlockSpec(memory_space=pltpu.VMEM)
    hbm = pl.BlockSpec(memory_space=pl.ANY)
    out = pl.pallas_call(
        fused,
        out_shape=jax.ShapeDtypeStruct((NSEC, LR * CH, COLS), BF16),
        in_specs=[vmem, vmem, hbm] + [vmem] * 6,
        out_specs=hbm,
        scratch_shapes=[
            pltpu.VMEM((NSEC + 1, LR * CH, COLS), BF16),
            pltpu.VMEM((NSEC, W_ROWS, 256), BF16),
            pltpu.VMEM((NSEC, NSP, 8, 512), BF16),
            pltpu.VMEM((NSEC, NSP, 8, 512), BF16),
            pltpu.VMEM((NSEC, NSP, 4, 8, 128), BF16),
            pltpu.VMEM((NSEC, 4, NSP, 8, 128), BF16),
            pltpu.VMEM((512, 128), BF16),
            pltpu.VMEM((512, 512), BF16),
            pltpu.VMEM((256, 128), BF16),
            pltpu.VMEM((512, 512), BF16),
            pltpu.VMEM((256, 256), BF16),
            pltpu.SemaphoreType.DMA((NSEC,)),
            pltpu.SemaphoreType.DMA((NSEC,)),
            pltpu.SemaphoreType.DMA((NSEC,)),
            pltpu.SemaphoreType.DMA((NSEC,)),
            pltpu.SemaphoreType.DMA((NSEC,)),
            pltpu.SemaphoreType.DMA((NSEC,)),
            pltpu.SemaphoreType.DMA((NSEC,)),
            pltpu.SemaphoreType.DMA,
        ],
        compiler_params=pltpu.CompilerParams(
            collective_id=0, has_side_effects=True, vmem_limit_bytes=60 << 20
        ),
        name="fused",
    )(feat, lift, w_all, fwt, e2, gi, gw, perm, rep)
    out = out.reshape(NSEC, LR, CH, COLS).transpose(0, 2, 1, 3)
    return out[None]


def solution(mesh):
    in_specs = (
        P(None, None, "space", None),
        P(),
        P("section", "space", None, None, None),
        P("section", None, None),
        P("section", None),
    )
    out_specs = P("section", None, None, "space", None)
    return jax.shard_map(
        on_device, mesh=mesh, in_specs=in_specs, out_specs=out_specs, check_vma=False
    )
```

time: 927 us -> 369 us (0.40)
  the two profiles are of different devices: /device:TPU:10 before, /device:TPU:7 now
where the time goes in v1:
time: 369 us; the launch traced here: 368 us
  Pallas kernels  189 us (51%)
  waiting for transfers between devices  86.3 us (23%)
  local copies, waits for them, and re-layouts  78.4 us (21%)
  between operations  13.5 us (4%)
    pallas_call x1, Pallas kernels, on_device(): pl.pallas_call(fused, out_shape=jax.ShapeDtypeStruct((NSEC, LR * CH, COLS...  189 us
    all_gather x1, waiting for transfers between devices, on_device(): w_all = lax.all_gather(own, 'section')  86.3 us
    transpose x1, local copies, waits for them, and re-layouts, pack_weights(): s = s.transpose(1, 5, 3, 4, 2, 0, 6).reshape(4096, 256)  25.7 us
    another operation x1, local copies, waits for them, and re-layouts, pack_weights(): s = spec_w.reshape(LM, 8, 2, 8, CH, 2, CH)  14.7 us
    reshape x1, local copies, waits for them, and re-layouts, on_device(): out = out.reshape(NSEC, LR, CH, COLS).transpose(0, 2, 1, 3)  12.1 us
    reshape x1, local copies, waits for them, and re-layouts, pack_weights(): s = s.transpose(1, 5, 3, 4, 2, 0, 6).reshape(4096, 256)  11.8 us
    unnamed x7, local copies, waits for them, and re-layouts  7.39 us
  transfers between devices with their start and end apart: 1, of which 1 were waited for; matrix products, arithmetic and copies ran while one was open for 0% of the time, Pallas kernels for 0%

profile of v1, /device:TPU:7, one launch (start us, length us, event | category | flops | bytes accessed | tf_op | source)
XLA Modules:
  0.0 367.7 jit_solution(65595499651726510)
XLA Ops:
  6.5 0.0 all-gather.3.cloned.1.call-start
  6.5 7.4 %copy.25 = bf16[1,4,128,32,64]{4,3,2,1,0:T(8,128)(2,1)} copy(bf16[1,4,128,32,64]{2,4,3,1,0:T(8,128)(2,1)} %param.13) | data formatting | bytes 4194304 | tf_op args[2]
  13.9 14.7 %reshape_squeeze.3 = bf16[4,8,2,8,32,2,32]{6,5,4,3,2,1,0:T(2,128)(2,1)} reshape(bf16[1,4,128,32,64]{4,3,2,1,0:T(8,128)(2,1)} %copy.25) | data formatting | bytes 4194304 | tf_op jit(solution)/shard_map/reshape;squeeze | solution.py:320
  28.6 25.7 %copy.26 = bf16[8,2,8,32,2,4,32]{3,2,1,0,6,5,4:T(8,128)(2,1)} copy(bf16[8,2,8,32,2,4,32]{6,1,3,2,4,0,5:T(2,128)(2,1)} %bitcast.25) | data formatting | bytes 4194304 | tf_op jit(solution)/shard_map/transpose | solution.py:321
  54.3 0.0 copy-start
  54.3 0.0 copy-start.1
  54.3 0.0 copy-start.2
  54.3 11.8 %reshape.28 = bf16[4096,256]{0,1:T(8,128)(2,1)} reshape(bf16[8,2,8,32,2,4,32]{3,2,1,0,6,5,4:T(8,128)(2,1)} %copy.26) | data formatting | bytes 4194304 | tf_op jit(solution)/shard_map/reshape | solution.py:321
  66.0 0.0 copy-done
  66.0 0.0 copy-done.1
  66.1 3.5 concatenate.3
  69.6 2.4 copy.27
  71.9 0.0 all-gather.3.cloned.1.call-update
  72.0 0.0 copy-done.2
  72.0 0.1 broadcast_multiply_fusion
  72.1 0.2 mul.20
  72.3 0.8 copy.28.lift
  73.0 86.3 %all-gather.3.cloned.1.call-done = bf16[33280,256]{1,0:T(8,128)(2,1)} async-done(((bf16[4160,256]{1,0:T(8,128)(2,1)}), bf16[33280,256]{1,0:T(8,128)(2,1)}) %all-gather.3.cloned.1.call-update) | async-done | bytes 17039376 | tf_op jit(solution)/shard_map/all_gather | solution.py:333
  159.3 189.4 %fused.1 = bf16[8,512,1024]{2,1,0:T(8,128)(2,1)} custom-call(bf16[8,32,1024]{2,1,0:T(8,128)(2,1)} %bitcast.28, bf16[512,32]{1,0:T(8,128)(2,1)} %copy.28.lift, bf16[8,4160,256]{2,1,0:T(8,128)(2,1)} %bitcast.27, bf16[128,1024]{1,0:T(8,128)(2,1)} %constant.12.clone.fwt, bf16[512,512]{1,0:T(8,128)(2,1)} %constant.13.clone.e2, ...), custom_call_target="tpu_custom_call" | custom-call | tf_op jit(solution)/shard_map/fused/pallas_call | solution.py:336
  348.7 12.1 %copy.31 = bf16[8,16,32,1024]{3,1,2,0:T(8,128)(2,1)} copy(bf16[8,16,32,1024]{3,2,1,0:T(8,128)(2,1)} %bitcast.26) | data formatting | bytes 16777216 | tf_op jit(solution)/shard_map/reshape | solution.py:367
  (3 shorter events, 0.0 us)
Async XLA Ops:
  6.5 152.8 %all-gather.3.cloned.1.call-start = ((), (), s32[]{:S(2)}) async-start(), calls=%async_computation | async-start | bytes 19169280 | tf_op jit(solution)/shard_map/all_gather | solution.py:333
  54.3 11.8 %copy-start = (bf16[1,32,32]{2,1,0:T(8,128)(2,1)S(1)}, bf16[1,32,32]{2,1,0:T(8,128)(2,1)}, u32[]{:S(2)}) copy-start(bf16[1,32,32]{2,1,0:T(8,128)(2,1)} %param.14) | copy-start | bytes 6148
  54.3 11.8 %copy-start.1 = (bf16[1,32]{1,0:T(2,128)(2,1)S(1)}, bf16[1,32]{1,0:T(2,128)(2,1)}, u32[]{:S(2)}) copy-start(bf16[1,32]{1,0:T(2,128)(2,1)} %param.15) | copy-start | bytes 196
  54.3 17.7 %copy-start.2 = (bf16[2,32]{1,0:T(2,128)(2,1)S(1)}, bf16[2,32]{1,0:T(2,128)(2,1)}, u32[]{:S(2)}) copy-start(bf16[2,32]{1,0:T(2,128)(2,1)} %param.12) | copy-start | bytes 388
Sparse Core Ops, SparseCore 0:
  72.1 87.1 all-gather.2
